TPU v7x, 32 devices: a whole 2x2x4 slice. The times are simulated.
32 devices in a mesh: dp: 2 (over x), expert: 16 (over z, y, core).
Axes of the slice: x: 2, y: 2, z: 4, core: 2. Of those that a mesh axis runs over, the one named last changes fastest.
Arguments:
- saved_inputs: bfloat16 [1024, 3584], P('expert'), may hold values from -6 to 6
- output_grad: bfloat16 [1024, 3584], P('expert'), may hold values from -6 to 6
- routes: int32 [1024, 8], P('expert'), may hold values from 0 to 15, all different within a row; in each aligned block of 64 rows (0 to 63, 64 to 127, ...) at most 36 rows name the same one
- route_gates: bfloat16 [1024, 8], P('expert'), may hold values from 0.099609375 to 1
- expert_gate: bfloat16 [16, 3584, 1024], P('expert', None, 'dp'), may hold values from -0.09375 to 0.09375
- expert_up: bfloat16 [16, 3584, 1024], P('expert', None, 'dp'), may hold values from -0.09375 to 0.09375
- expert_down: bfloat16 [16, 1024, 3584], P('expert', 'dp'), may hold values from -0.1875 to 0.1875
- proj_basis: bfloat16 [16, 1024, 128], P('expert', 'dp'), may hold values from -0.1875 to 0.1875
Outputs:
- input_grad: bfloat16 [1024, 3584], P('expert', 'dp')
- projected: float32 [16, 3584, 3, 128], P('expert', 'dp')
Inputs may be any that keep to these rules, and one draw needn't show every extreme that they name: Within each aligned block of 64 tokens no expert is named by more than 36 routes, and in every draw some expert is named by exactly 36.
All inputs are finite; a program needn't handle non-finite values.
Results may differ from a plain program's by a relative error of at most 0.009.
Values may be sent and summed in bfloat16 or wider, within the bound.
A program may use at most 128 MiB of HBM per device.

v0:
```python
import jax
import jax.numpy as jnp
from jax import lax
from jax.sharding import PartitionSpec as P


def slot_form(
    saved_inputs, output_grad, routes, route_gates, expert_gate, expert_up, expert_down, proj_basis
):
    token_count, model_width = saved_inputs.shape
    top_count = routes.shape[1]
    expert_count = lax.axis_size("expert")
    group_count = lax.axis_size("dp")
    capacity = token_count * top_count * 9 // (8 * expert_count)
    slot_count = expert_count * capacity
    column_width = model_width // group_count
    route_count = token_count * top_count
    flat_routes = routes.reshape(-1)
    one_hot = (flat_routes[:, None] == jnp.arange(expert_count, dtype=jnp.int32)[None, :]).astype(
        jnp.int32
    )
    earlier = jnp.sum((jnp.cumsum(one_hot, axis=0) - one_hot) * one_hot, axis=1)
    target_slot = flat_routes * capacity + earlier
    slot_owner = (
        jnp.full((slot_count,), route_count, jnp.int32)
        .at[target_slot]
        .set(jnp.arange(route_count, dtype=jnp.int32))
    )
    filled = slot_owner < route_count
    safe_route = jnp.minimum(slot_owner, route_count - 1)
    source_token = safe_route // top_count
    zero_half = jnp.zeros((), jnp.bfloat16)
    gate_slots = jnp.where(filled, route_gates.reshape(-1)[safe_route], zero_half).reshape(
        expert_count, capacity
    )
    token_map = (
        (source_token[None, :] == jnp.arange(token_count, dtype=jnp.int32)[:, None])
        & filled[None, :]
    ).astype(jnp.bfloat16)
    contract_first = (((0,), (0,)), ((), ()))

    def to_slots(source_rows):
        picked = lax.dot_general(
            token_map, source_rows, contract_first, preferred_element_type=jnp.float32
        ).astype(jnp.bfloat16)
        return picked.reshape(expert_count, capacity * source_rows.shape[1])

    recv_inputs, recv_grads, recv_gates = (
        lax.all_to_all(to_slots(saved_inputs), "expert", split_axis=0, concat_axis=0, tiled=True),
        lax.all_to_all(to_slots(output_grad), "expert", split_axis=0, concat_axis=0, tiled=True),
        lax.all_to_all(gate_slots, "expert", split_axis=0, concat_axis=0, tiled=True),
    )
    input_rows = recv_inputs.reshape(slot_count, model_width)
    grad_rows = recv_grads.reshape(slot_count, model_width)
    gain = recv_gates.reshape(slot_count, 1).astype(jnp.float32)
    gate_w = expert_gate[0]
    up_w = expert_up[0]
    down_w = expert_down[0]
    basis = proj_basis[0]
    rank_width = basis.shape[1]
    contract_last = (((1,), (1,)), ((), ()))
    pre_gate = jnp.dot(input_rows, gate_w, preferred_element_type=jnp.float32)
    pre_up = jnp.dot(input_rows, up_w, preferred_element_type=jnp.float32)
    grad_hidden = lax.dot_general(
        grad_rows, down_w, contract_last, preferred_element_type=jnp.float32
    )
    sigma = jax.nn.sigmoid(pre_gate)
    silu_val = pre_gate * sigma
    scaled = gain * grad_hidden
    grad_up = (scaled * silu_val).astype(jnp.bfloat16)
    grad_gate = (scaled * pre_up * sigma * (1.0 + pre_gate * (1.0 - sigma))).astype(jnp.bfloat16)
    hidden = (silu_val * pre_up).astype(jnp.bfloat16)
    part_rows = (
        lax.dot_general(grad_gate, gate_w, contract_last, preferred_element_type=jnp.float32)
        + lax.dot_general(grad_up, up_w, contract_last, preferred_element_type=jnp.float32)
    ).astype(jnp.bfloat16)
    coef_gate = jnp.dot(grad_gate, basis, preferred_element_type=jnp.float32).astype(jnp.bfloat16)
    coef_up = jnp.dot(grad_up, basis, preferred_element_type=jnp.float32).astype(jnp.bfloat16)
    coef_down = (gain * jnp.dot(hidden, basis, preferred_element_type=jnp.float32)).astype(
        jnp.bfloat16
    )
    coef_pair = jnp.concatenate([coef_gate, coef_up], axis=1)
    front = lax.dot_general(
        input_rows, coef_pair, contract_first, preferred_element_type=jnp.float32
    )
    rear = lax.dot_general(grad_rows, coef_down, contract_first, preferred_element_type=jnp.float32)
    summed_terms = lax.psum_scatter(
        jnp.concatenate([front, rear], axis=1).astype(jnp.bfloat16),
        "dp",
        scatter_dimension=0,
        tiled=True,
    ).astype(jnp.float32)
    projected = summed_terms.reshape(1, column_width, 3, rank_width)
    returned = lax.all_to_all(
        part_rows.reshape(expert_count, capacity * model_width),
        "expert",
        split_axis=0,
        concat_axis=0,
        tiled=True,
    )
    spread = jnp.dot(
        token_map, returned.reshape(slot_count, model_width), preferred_element_type=jnp.float32
    )
    token_grad = lax.psum_scatter(
        spread.astype(jnp.bfloat16), "dp", scatter_dimension=1, tiled=True
    )
    return (token_grad, projected)


def dense_form(
    saved_inputs, output_grad, routes, route_gates, expert_gate, expert_up, expert_down, proj_basis
):
    model_width = saved_inputs.shape[1]
    expert_count = lax.axis_size("expert")
    group_count = lax.axis_size("dp")
    column_width = model_width // group_count
    experts = jnp.arange(expert_count, dtype=jnp.int32)
    chosen = routes[:, :, None] == experts[None, None, :]
    gate_table = jnp.sum(
        jnp.where(chosen, route_gates.astype(jnp.float32)[:, :, None], 0.0), axis=1
    ).astype(jnp.bfloat16)
    all_gates = lax.all_gather(gate_table, "expert", axis=0, tiled=True)
    input_rows = lax.all_gather(saved_inputs, "expert", axis=0, tiled=True)
    grad_rows = lax.all_gather(output_grad, "expert", axis=0, tiled=True)
    own = experts == lax.axis_index("expert")
    gain = jnp.sum(
        jnp.where(own[None, :], all_gates.astype(jnp.float32), 0.0), axis=1, keepdims=True
    )
    gate_w = expert_gate[0]
    up_w = expert_up[0]
    down_w = expert_down[0]
    basis = proj_basis[0]
    rank_width = basis.shape[1]
    contract_first = (((0,), (0,)), ((), ()))
    contract_last = (((1,), (1,)), ((), ()))
    pre_gate = jnp.dot(input_rows, gate_w, preferred_element_type=jnp.float32)
    pre_up = jnp.dot(input_rows, up_w, preferred_element_type=jnp.float32)
    grad_hidden = lax.dot_general(
        grad_rows, down_w, contract_last, preferred_element_type=jnp.float32
    )
    sigma = jax.nn.sigmoid(pre_gate)
    silu_val = pre_gate * sigma
    scaled = gain * grad_hidden
    grad_up = (scaled * silu_val).astype(jnp.bfloat16)
    grad_gate = (scaled * pre_up * sigma * (1.0 + pre_gate * (1.0 - sigma))).astype(jnp.bfloat16)
    hidden = (silu_val * pre_up).astype(jnp.bfloat16)
    part_rows = (
        lax.dot_general(grad_gate, gate_w, contract_last, preferred_element_type=jnp.float32)
        + lax.dot_general(grad_up, up_w, contract_last, preferred_element_type=jnp.float32)
    ).astype(jnp.bfloat16)
    own_rows = lax.psum_scatter(part_rows, "expert", scatter_dimension=0, tiled=True)
    token_grad = lax.psum_scatter(own_rows, "dp", scatter_dimension=1, tiled=True)
    coef_gate = jnp.dot(grad_gate, basis, preferred_element_type=jnp.float32).astype(jnp.bfloat16)
    coef_up = jnp.dot(grad_up, basis, preferred_element_type=jnp.float32).astype(jnp.bfloat16)
    coef_down = (gain * jnp.dot(hidden, basis, preferred_element_type=jnp.float32)).astype(
        jnp.bfloat16
    )
    coef_pair = jnp.concatenate([coef_gate, coef_up], axis=1)
    front = lax.dot_general(
        input_rows, coef_pair, contract_first, preferred_element_type=jnp.float32
    )
    rear = lax.dot_general(grad_rows, coef_down, contract_first, preferred_element_type=jnp.float32)
    summed_terms = lax.psum_scatter(
        jnp.concatenate([front, rear], axis=1).astype(jnp.bfloat16),
        "dp",
        scatter_dimension=0,
        tiled=True,
    ).astype(jnp.float32)
    projected = summed_terms.reshape(1, column_width, 3, rank_width)
    return (token_grad, projected)


def on_device(*arrays):
    if lax.axis_size("expert") <= 2 * arrays[2].shape[1]:
        return dense_form(*arrays)
    return slot_form(*arrays)


def solution(mesh):
    placed = (
        P("expert", None),
        P("expert", None),
        P("expert", None),
        P("expert", None),
        P("expert", None, "dp"),
        P("expert", None, "dp"),
        P("expert", "dp", None),
        P("expert", "dp", None),
    )
    return jax.shard_map(
        on_device,
        mesh=mesh,
        in_specs=placed,
        out_specs=(P("expert", "dp"), P("expert", "dp", None, None)),
        check_vma=False,
    )
```

profile of v0, /device:TPU:0, one launch (start us, length us, event | category | flops | bytes accessed | tf_op | source)
XLA Modules:
  0.0 331.8 jit_solution(12688891040194044894)
XLA Ops:
  7.2 0.7 all-gather.6.cloned.1.call-update
  8.0 0.7 all-gather.4.cloned.1.call-update
  8.7 0.7 convert_element_type.32
  9.4 0.7 select_reduce_fusion.1
  10.1 23.8 %all-gather = bf16[16,64,16]{1,2,0:T(8,128)(2,1)S(1)} all-gather(bf16[1,64,16]{1,2,0:T(8,128)(2,1)S(1)} %bitcast.44), channel_id=1, replica_groups=mesh['dp'=2,'expert'=16] {'expert'}, dimensions={0}, use_global_device_ids=true | all-gather | bytes 34816 | tf_op jit(solution)/shard_map/all_gather | solution.py:122
  33.9 0.1 reshape.23
  34.1 0.1 select_reduce_fusion
  34.1 46.7 %all-gather.6.cloned.1.call-done = bf16[1024,3584]{1,0:T(8,128)(2,1)} async-done(((bf16[64,3584]{1,0:T(8,128)(2,1)}), bf16[1024,3584]{1,0:T(8,128)(2,1)}) %all-gather.6.cloned.1.call-update) | async-done | bytes 7340048 | tf_op jit(solution)/shard_map/all_gather | solution.py:123
  80.8 9.5 %fusion.4 = f32[1024,512]{1,0:T(8,128)} fusion(bf16[1024,3584]{1,0:T(8,128)(2,1)} %all-gather.6.cloned.1.call-done, bf16[1,3584,512]{2,1,0:T(8,128)(2,1)} %param.12), kind=kOutput, calls=%fused_computation.7 | convolution fusion | flops 3758096384 | bytes 13107200 | tf_op jit(solution)/shard_map/dot_general | solution.py:136
  90.4 5.3 %fusion.7 = f32[1024,512]{1,0:T(8,128)} fusion(bf16[1024,3584]{1,0:T(8,128)(2,1)S(1)} %copy-done.1, bf16[1,3584,512]{2,1,0:T(8,128)(2,1)S(1)} %copy-done.3), kind=kOutput, calls=%fused_computation.10 | convolution fusion | flops 3758096384 | bytes 13107200 | tf_op jit(solution)/shard_map/dot_general | solution.py:137
  95.6 53.9 %all-gather.4.cloned.1.call-done = bf16[1024,3584]{1,0:T(8,128)(2,1)} async-done(((bf16[64,3584]{1,0:T(8,128)(2,1)}), bf16[1024,3584]{1,0:T(8,128)(2,1)}) %all-gather.4.cloned.1.call-update) | async-done | bytes 7340048 | tf_op jit(solution)/shard_map/all_gather | solution.py:124
  149.5 10.2 %multiply_convert_fusion.1 = (bf16[1024,512]{1,0:T(8,128)(2,1)S(1)}, bf16[1024,512]{1,0:T(8,128)(2,1)S(1)}) fusion(f32[1024]{0:T(1024)S(1)} %select_reduce_fusion, f32[1024,512]{1,0:T(8,128)} %fusion.4, f32[1024,512]{1,0:T(8,128)} %fusion.7, bf16[1024,3584]{1,0:T(8,128)(2,1)} %all-gather.4.cloned.1.call-done, bf16[1,512,3584]{2,1,0:T(8,128)(2,1)} %param.14), kind=kOutput, calls=%fused_computation.16 | convolution fusion | flops 3765436416 | bytes 17305600 | tf_op jit(solution)/shard_map/dot_general | solution.py:138
  159.7 7.4 %fusion.2 = f32[1024,3584]{1,0:T(8,128)} fusion(bf16[1024,512]{1,0:T(8,128)(2,1)S(1)} %get-tuple-element.11, bf16[1,3584,512]{2,1,0:T(8,128)(2,1)S(1)} %copy-done.2), kind=kOutput, calls=%fused_computation.5 | convolution fusion | flops 3758096384 | bytes 19398656 | tf_op jit(solution)/shard_map/dot_general | solution.py:148
  167.2 9.4 %add_convert_fusion = bf16[1024,3584]{1,0:T(8,128)(2,1)} fusion(f32[1024,3584]{1,0:T(8,128)} %fusion.2, bf16[1024,512]{1,0:T(8,128)(2,1)S(1)} %get-tuple-element.10, bf16[1,3584,512]{2,1,0:T(8,128)(2,1)S(1)} %copy-done.4), kind=kOutput, calls=%fused_computation | convolution fusion | flops 3765436416 | bytes 26738688 | tf_op jit(solution)/shard_map/dot_general | solution.py:149
  176.6 0.2 reduce-scatter.8.cloned.1.call-start
  176.8 0.5 convolution_convert_fusion.2
  177.3 0.5 convolution_convert_fusion.3
  177.8 5.2 %fusion = bf16[3584,256]{0,1:T(8,128)(2,1)S(1)} fusion(bf16[1024,3584]{1,0:T(8,128)(2,1)} %all-gather.6.cloned.1.call-done, bf16[1024,128]{0,1:T(8,128)(2,1)S(1)} %convolution_convert_fusion.2, bf16[1024,128]{0,1:T(8,128)(2,1)S(1)} %convolution_convert_fusion.3), kind=kOutput, calls=%fused_computation.2 | convolution fusion | flops 1881014272 | bytes 9699328 | tf_op jit(solution)/shard_map/dot_general | solution.py:159
  182.9 7.3 %fusion.1 = bf16[3584,128]{0,1:T(8,128)(2,1)S(1)} fusion(bf16[1024,3584]{1,0:T(8,128)(2,1)} %all-gather.4.cloned.1.call-done, f32[1024,512]{1,0:T(8,128)} %fusion.7, f32[1024,512]{1,0:T(8,128)} %fusion.4, f32[1024]{0:T(1024)S(1)} %select_reduce_fusion, bf16[1,512,128]{2,1,0:T(8,128)(2,1)S(1)} %copy-done), kind=kOutput, calls=%fused_computation.4 | convolution fusion | flops 1077608448 | bytes 12587008 | tf_op jit(solution)/shard_map/dot_general | solution.py:162
  190.3 1.7 pad_maximum_fusion
  192.1 75.0 %reduce-scatter.4.cloned.1.call-done = bf16[64,3584]{1,0:T(8,128)(2,1)} async-done(((bf16[1024,3584]{1,0:T(8,128)(2,1)}), bf16[64,3584]{1,0:T(8,128)(2,1)}) %reduce-scatter.4.cloned.1.call-update) | async-done | bytes 458768 | tf_op jit(solution)/shard_map/reduce_scatter | solution.py:151
  267.1 41.6 %reduce-scatter.8.cloned.1.call-done = bf16[1792,384]{0,1:T(8,128)(2,1)} async-done(((bf16[3584,384]{0,1:T(8,128)(2,1)}), bf16[1792,384]{0,1:T(8,128)(2,1)}) %reduce-scatter.8.cloned.1.call-update) | async-done | bytes 1376272 | tf_op jit(solution)/shard_map/reduce_scatter | solution.py:163
  308.7 2.9 copy.21
  311.6 13.7 %reduce-scatter.6.cloned.1.call-done = bf16[64,1792]{1,0:T(8,128)(2,1)} async-done(((bf16[64,3584]{1,0:T(8,128)(2,1)}), bf16[64,1792]{1,0:T(8,128)(2,1)}) %reduce-scatter.6.cloned.1.call-update) | async-done | bytes 229392 | tf_op jit(solution)/shard_map/reduce_scatter | solution.py:152
  (19 shorter events, 0.3 us)
Async XLA Ops:
  7.2 169.6 %copy-start = (bf16[1,512,128]{2,1,0:T(8,128)(2,1)S(1)}, bf16[1,512,128]{2,1,0:T(8,128)(2,1)}, u32[]{:S(2)}) copy-start(bf16[1,512,128]{2,1,0:T(8,128)(2,1)} %param.15) | copy-start | bytes 393220
  7.2 73.6 %all-gather.6.cloned.1.call-start = ((), (), s32[]{:S(2)}) async-start(), calls=%async_computation.4 | async-start | bytes 7798784 | tf_op jit(solution)/shard_map/all_gather | solution.py:123
  7.9 141.6 %all-gather.4.cloned.1.call-start = ((), (), s32[]{:S(2)}) async-start(), calls=%async_computation.3 | async-start | bytes 7798784 | tf_op jit(solution)/shard_map/all_gather | solution.py:124
  8.7 258.4 %reduce-scatter.4.cloned.1.call-start = ((), (), s32[]{:S(2)}) async-start(), calls=%async_computation.5 | async-start | bytes 7798784 | tf_op jit(solution)/shard_map/reduce_scatter | solution.py:151
  80.8 9.5 %copy-start.1 = (bf16[1024,3584]{1,0:T(8,128)(2,1)S(1)}, bf16[1024,3584]{1,0:T(8,128)(2,1)}, u32[]{:S(2)}) copy-start(bf16[1024,3584]{1,0:T(8,128)(2,1)} %all-gather.6.cloned.1.call-done) | copy-start | bytes 22020100
  80.8 9.5 %copy-start.3 = (bf16[1,3584,512]{2,1,0:T(8,128)(2,1)S(1)}, bf16[1,3584,512]{2,1,0:T(8,128)(2,1)}, u32[]{:S(2)}) copy-start(bf16[1,3584,512]{2,1,0:T(8,128)(2,1)} %param.13) | copy-start | bytes 11010052
  149.5 10.2 %copy-start.2 = (bf16[1,3584,512]{2,1,0:T(8,128)(2,1)S(1)}, bf16[1,3584,512]{2,1,0:T(8,128)(2,1)}, u32[]{:S(2)}) copy-start(bf16[1,3584,512]{2,1,0:T(8,128)(2,1)} %param.12) | copy-start | bytes 11010052
  159.7 7.4 %copy-start.4 = (bf16[1,3584,512]{2,1,0:T(8,128)(2,1)S(1)}, bf16[1,3584,512]{2,1,0:T(8,128)(2,1)}, u32[]{:S(2)}) copy-start(bf16[1,3584,512]{2,1,0:T(8,128)(2,1)} %param.13) | copy-start | bytes 11010052
  176.6 132.1 %reduce-scatter.8.cloned.1.call-start = ((), (), s32[]{:S(2)}) async-start(), calls=%async_computation.7 | async-start | bytes 4128768 | tf_op jit(solution)/shard_map/reduce_scatter | solution.py:163
  192.0 133.3 %reduce-scatter.6.cloned.1.call-start = ((), (), s32[]{:S(2)}) async-start(), calls=%async_computation.6 | async-start | bytes 688128 | tf_op jit(solution)/shard_map/reduce_scatter | solution.py:152
Sparse Core Ops, SparseCore 0:
  10.3 70.4 all-gather.5
  83.1 66.4 all-gather.3
  176.7 90.3 reduce-scatter.3
  269.8 38.8 reduce-scatter.7
  311.4 13.9 reduce-scatter.5
where the time goes:
time: 332 us
  waiting for transfers between devices  232 us (70%)
  matrix products  55.2 us (17%)
  blocking collectives  23.8 us (7%)
  between operations  13.9 us (4%)
    reduce_scatter x1, waiting for transfers between devices, dense_form(): lax.psum_scatter(part_rows, 'expert', scatter_dimension=0, tiled=True)  75 us
    all_gather x1, waiting for transfers between devices, dense_form(): grad_rows = lax.all_gather(output_grad, 'expert', axis=0, tiled=True)  53.9 us
    all_gather x1, waiting for transfers between devices, dense_form(): input_rows = lax.all_gather(saved_inputs, 'expert', axis=0, tiled=True)  46.7 us
    reduce_scatter x1, waiting for transfers between devices, dense_form(): lax.psum_scatter(jnp.concatenate([front, rear], axis=1).astype(jnp.bfloat...  41.6 us
    all_gather x1, blocking collectives, dense_form(): all_gates = lax.all_gather(gate_table, 'expert', axis=0, tiled=True)  23.8 us
    reduce_scatter x1, waiting for transfers between devices, dense_form(): lax.psum_scatter(own_rows, 'dp', scatter_dimension=1, tiled=True)  13.7 us
    dot_general x1, matrix products, dense_form(): lax.dot_general(grad_rows, down_w, contract_last, preferred_element_type=...  10.2 us
    dot_general x1, matrix products, dense_form(): pre_gate = jnp.dot(input_rows, gate_w, preferred_element_type=jnp.float32)  9.54 us
  transfers between devices with their start and end apart: 5, of which 5 were waited for; matrix products, arithmetic and copies ran while one was open for 10% of the time, Pallas kernels for 0%

commit v1 on v0

--- a/solution.py
+++ b/solution.py
@@ -120,7 +120,15 @@
         jnp.where(chosen, route_gates.astype(jnp.float32)[:, :, None], 0.0), axis=1
     ).astype(jnp.bfloat16)
     all_gates = lax.all_gather(gate_table, "expert", axis=0, tiled=True)
-    input_rows = lax.all_gather(saved_inputs, "expert", axis=0, tiled=True)
+    ways, here, hop = (lax.axis_size("expert"), lax.axis_index("expert"), saved_inputs.shape[0])
+    line, have = (saved_inputs, 1)
+    while have < ways:
+        line = jnp.concatenate(
+            [line, lax.ppermute(line, "expert", [(d, (d - have) % ways) for d in range(ways)])],
+            axis=0,
+        )
+        have = 2 * have
+    input_rows = jnp.roll(line, here * hop, axis=0)
     grad_rows = lax.all_gather(output_grad, "expert", axis=0, tiled=True)
     own = experts == lax.axis_index("expert")
     gain = jnp.sum(

time: 332 us -> 505 us (1.52)
  waiting for transfers between devices: 232 us -> 319 us
  blocking collectives: 23.8 us -> 97.3 us
  local copies, waits for them, and re-layouts: 3.04 us -> 11 us
  starting transfers between devices: 0.38 us -> 7.46 us
  matrix products: 55.2 us -> 50 us
    ppermute x0 -> x4, waiting for transfers between devices: none -> 173 us  [dense_form(): lax.ppermute(line, 'expert', [(d, (d - have) % ways) for d in range(ways)])]
    all_gather x1, blocking collectives: 23.8 us -> 97.3 us  [dense_form(): all_gates = lax.all_gather(gate_table, 'expert', axis=0, tiled=True)]
    all_gather x1, waiting for transfers between devices: 53.9 us -> 0.01 us  [dense_form(): grad_rows = lax.all_gather(output_grad, 'expert', axis=0, tiled=True)]
    all_gather x1 -> x0, waiting for transfers between devices: 46.7 us -> none  [dense_form(): input_rows = lax.all_gather(saved_inputs, 'expert', axis=0, tiled=True)]
    reduce_scatter x1, waiting for transfers between devices: 75 us -> 89.4 us  [dense_form(): lax.psum_scatter(part_rows, 'expert', scatter_dimension=0, tiled=True)]
    ppermute x0 -> x4, starting transfers between devices: none -> 7.12 us  [dense_form(): lax.ppermute(line, 'expert', [(d, (d - have) % ways) for d in range(ways)])]
    unnamed x11 -> x32, local copies, waits for them, and re-layouts: 2.93 us -> 8.5 us
  transfers between devices with their start and end apart: 5 -> 8, of which waited for: 5 -> 7; matrix products, arithmetic and copies ran while one was open for 10% -> 8% of each run, Pallas kernels for 0% -> 0%
where the time goes in v1:
time: 505 us
  waiting for transfers between devices  319 us (63%)
  blocking collectives  97.3 us (19%)
  matrix products  50 us (10%)
  between operations  14 us (3%)
  local copies, waits for them, and re-layouts  11 us (2%)
  starting transfers between devices  7.46 us (1%)
  other arithmetic  6.27 us (1%)
    ppermute x4, waiting for transfers between devices, dense_form(): lax.ppermute(line, 'expert', [(d, (d - have) % ways) for d in range(ways)])  173 us
    all_gather x1, blocking collectives, dense_form(): all_gates = lax.all_gather(gate_table, 'expert', axis=0, tiled=True)  97.3 us
    reduce_scatter x1, waiting for transfers between devices, dense_form(): lax.psum_scatter(part_rows, 'expert', scatter_dimension=0, tiled=True)  89.4 us
    reduce_scatter x1, waiting for transfers between devices, dense_form(): lax.psum_scatter(jnp.concatenate([front, rear], axis=1).astype(jnp.bfloat...  41.7 us
    reduce_scatter x1, waiting for transfers between devices, dense_form(): lax.psum_scatter(own_rows, 'dp', scatter_dimension=1, tiled=True)  13.7 us
    dot_general x1, matrix products, dense_form(): lax.dot_general(grad_rows, down_w, contract_last, preferred_element_type=...  10.2 us
  transfers between devices with their start and end apart: 8, of which 7 were waited for; matrix products, arithmetic and copies ran while one was open for 8% of the time, Pallas kernels for 0%

profile of v1, /device:TPU:0, one launch (start us, length us, event | category | flops | bytes accessed | tf_op | source)
XLA Modules:
  0.0 504.9 jit_solution(10240183513865048776)
XLA Ops:
  8.0 5.5 %collective-permute-start = (bf16[64,3584]{1,0:T(8,128)(2,1)}, bf16[64,3584]{1,0:T(8,128)(2,1)S(1)}, u32[]{:S(2)}, u32[]{:S(2)}) collective-permute-start(bf16[64,3584]{1,0:T(8,128)(2,1)} %param.8), channel_id=1, source_target_pairs={{0,15},{1,0},{2,1},{3,2},{4,3},{5,4},{6,5},{7,6},{8,7},{9,8},{10,9... | collective-permute-start | bytes 1376264 | tf_op jit(solution)/shard_map/ppermute | solution.py:127
  13.5 6.3 %collective-permute-done = bf16[64,3584]{1,0:T(8,128)(2,1)S(1)} collective-permute-done((bf16[64,3584]{1,0:T(8,128)(2,1)}, bf16[64,3584]{1,0:T(8,128)(2,1)S(1)}, u32[]{:S(2)}, u32[]{:S(2)}) %collective-permute-start) | collective-permute-done | bytes 458784 | tf_op jit(solution)/shard_map/ppermute | solution.py:127
  19.8 1.3 pad_maximum_fusion.3
  21.7 33.4 %collective-permute-done.1 = bf16[128,3584]{1,0:T(8,128)(2,1)S(1)} collective-permute-done((bf16[128,3584]{1,0:T(8,128)(2,1)S(1)}, bf16[128,3584]{1,0:T(8,128)(2,1)S(1)}, u32[]{:S(2)}, u32[]{:S(2)}) %collective-permute-start.1) | collective-permute-done | bytes 917536 | tf_op jit(solution)/shard_map/ppermute | solution.py:127
  55.1 1.1 pad_maximum_fusion.2
  57.3 71.1 %collective-permute-done.2 = bf16[256,3584]{1,0:T(8,128)(2,1)S(1)} collective-permute-done((bf16[256,3584]{1,0:T(8,128)(2,1)S(1)}, bf16[256,3584]{1,0:T(8,128)(2,1)S(1)}, u32[]{:S(2)}, u32[]{:S(2)}) %collective-permute-start.2) | collective-permute-done | bytes 1835040 | tf_op jit(solution)/shard_map/ppermute | solution.py:127
  128.4 2.0 pad_maximum_fusion
  130.5 97.3 %all-gather = bf16[16,64,16]{1,2,0:T(8,128)(2,1)S(1)} all-gather(bf16[1,64,16]{1,2,0:T(8,128)(2,1)S(1)} %bitcast.39), channel_id=1, replica_groups=mesh['dp'=2,'expert'=16] {'expert'}, dimensions={0}, use_global_device_ids=true | all-gather | bytes 34816 | tf_op jit(solution)/shard_map/all_gather | solution.py:122
  229.3 62.5 %collective-permute-done.3 = bf16[512,3584]{1,0:T(8,128)(2,1)} collective-permute-done((bf16[512,3584]{1,0:T(8,128)(2,1)}, bf16[512,3584]{1,0:T(8,128)(2,1)}, u32[]{:S(2)}, u32[]{:S(2)}) %collective-permute-start.3) | collective-permute-done | bytes 3670048 | tf_op jit(solution)/shard_map/ppermute | solution.py:127
  291.8 2.3 constant_dynamic-update-slice_fusion.5
  294.3 2.4 constant_dynamic-update-slice_fusion
  297.5 5.8 %fusion.4 = f32[1024,512]{1,0:T(8,128)} fusion(bf16[2048,3584]{1,0:T(8,128)(2,1)S(1)} %constant_dynamic-update-slice_fusion, s32[]{:T(128)S(6)} %select_n.24, bf16[1,3584,512]{2,1,0:T(8,128)(2,1)S(1)} %copy-done.9), kind=kOutput, calls=%fused_computation.5 | convolution fusion | flops 3758096384 | bytes 13107204 | tf_op jit(solution)/shard_map/dot_general | solution.py:145
  303.2 1.1 copy-done.4
  304.3 5.3 %fusion.2 = f32[1024,512]{1,0:T(8,128)} fusion(bf16[2048,3584]{1,0:T(8,128)(2,1)S(1)} %constant_dynamic-update-slice_fusion, s32[]{:T(128)S(6)} %select_n.24, bf16[1,3584,512]{2,1,0:T(8,128)(2,1)S(1)} %copy-done.7), kind=kOutput, calls=%fused_computation.3 | convolution fusion | flops 3758096384 | bytes 13107204 | tf_op jit(solution)/shard_map/dot_general | solution.py:144
  309.6 10.2 %multiply_convert_fusion.1 = (bf16[1024,512]{1,0:T(8,128)(2,1)S(1)}, bf16[1024,512]{1,0:T(8,128)(2,1)S(1)}) fusion(f32[1024]{0:T(1024)S(1)} %select_reduce_fusion, f32[1024,512]{1,0:T(8,128)} %fusion.2, f32[1024,512]{1,0:T(8,128)} %fusion.4, bf16[1024,3584]{1,0:T(8,128)(2,1)} %all-gather.3.cloned.1.call-done, bf16[1,512,3584]{2,1,0:T(8,128)(2,1)} %param.14), kind=kOutput, calls=%fused_computation.20 | convolution fusion | flops 3765436416 | bytes 17305600 | tf_op jit(solution)/shard_map/dot_general | solution.py:146
  319.7 7.3 %fusion.10 = f32[1024,3584]{1,0:T(8,128)} fusion(bf16[1024,512]{1,0:T(8,128)(2,1)S(1)} %get-tuple-element.11, bf16[1,3584,512]{2,1,0:T(8,128)(2,1)S(1)} %copy-done.8), kind=kOutput, calls=%fused_computation.11 | convolution fusion | flops 3758096384 | bytes 19398656 | tf_op jit(solution)/shard_map/dot_general | solution.py:156
  327.0 9.2 %add_convert_fusion = bf16[1024,3584]{1,0:T(8,128)(2,1)} fusion(f32[1024,3584]{1,0:T(8,128)} %fusion.10, bf16[1024,512]{1,0:T(8,128)(2,1)S(1)} %get-tuple-element.10, bf16[1,3584,512]{2,1,0:T(8,128)(2,1)S(1)} %copy-done.10), kind=kOutput, calls=%fused_computation | convolution fusion | flops 3765436416 | bytes 26738688 | tf_op jit(solution)/shard_map/dot_general | solution.py:157
  337.4 5.1 %fusion.6 = bf16[3584,256]{0,1:T(8,128)(2,1)S(1)} fusion(bf16[2048,3584]{1,0:T(8,128)(2,1)} %copy-done.4, s32[]{:T(128)S(6)} %select_n.24, bf16[1024,128]{0,1:T(8,128)(2,1)S(1)} %convolution_convert_fusion.1, bf16[1024,128]{0,1:T(8,128)(2,1)S(1)} %convolution_convert_fusion.2), kind=kOutput, calls=%fused_computation.7 | convolution fusion | flops 1881014272 | bytes 9699332 | tf_op jit(solution)/shard_map/dot_general | solution.py:167
  342.6 6.3 %fusion.9 = bf16[3584,128]{0,1:T(8,128)(2,1)S(1)} fusion(bf16[1024,3584]{1,0:T(8,128)(2,1)} %all-gather.3.cloned.1.call-done, f32[1024,512]{1,0:T(8,128)} %fusion.4, f32[1024,512]{1,0:T(8,128)} %fusion.2, f32[1024]{0:T(1024)S(1)} %select_reduce_fusion, bf16[1,512,128]{2,1,0:T(8,128)(2,1)S(1)} %copy-done), kind=kOutput, calls=%fused_computation.9 | convolution fusion | flops 1077608448 | bytes 12587008 | tf_op jit(solution)/shard_map/dot_general | solution.py:170
  348.9 1.7 pad_maximum_fusion.1
  350.7 89.4 %reduce-scatter.4.cloned.1.call-done = bf16[64,3584]{1,0:T(8,128)(2,1)} async-done(((bf16[1024,3584]{1,0:T(8,128)(2,1)}), bf16[64,3584]{1,0:T(8,128)(2,1)}) %reduce-scatter.4.cloned.1.call-update) | async-done | bytes 458768 | tf_op jit(solution)/shard_map/reduce_scatter | solution.py:159
  440.1 41.7 %reduce-scatter.8.cloned.1.call-done = bf16[1792,384]{0,1:T(8,128)(2,1)} async-done(((bf16[3584,384]{0,1:T(8,128)(2,1)}), bf16[1792,384]{0,1:T(8,128)(2,1)}) %reduce-scatter.8.cloned.1.call-update) | async-done | bytes 1376272 | tf_op jit(solution)/shard_map/reduce_scatter | solution.py:171
  481.8 2.9 copy.21
  484.7 13.7 %reduce-scatter.6.cloned.1.call-done = bf16[64,1792]{1,0:T(8,128)(2,1)} async-done(((bf16[64,3584]{1,0:T(8,128)(2,1)}), bf16[64,1792]{1,0:T(8,128)(2,1)}) %reduce-scatter.6.cloned.1.call-update) | async-done | bytes 229392 | tf_op jit(solution)/shard_map/reduce_scatter | solution.py:160
  (49 shorter events, 6.1 us)
Async XLA Ops:
  7.2 329.3 %copy-start = (bf16[1,512,128]{2,1,0:T(8,128)(2,1)S(1)}, bf16[1,512,128]{2,1,0:T(8,128)(2,1)}, u32[]{:S(2)}) copy-start(bf16[1,512,128]{2,1,0:T(8,128)(2,1)} %param.15) | copy-start | bytes 393220
  7.2 121.2 %copy-start.1 = (bf16[64,3584]{1,0:T(8,128)(2,1)S(1)}, bf16[64,3584]{1,0:T(8,128)(2,1)}, u32[]{:S(2)}) copy-start(bf16[64,3584]{1,0:T(8,128)(2,1)} %param.8) | copy-start | bytes 1376260
  7.2 302.4 %all-gather.3.cloned.1.call-start = ((), (), s32[]{:S(2)}) async-start(), calls=%async_computation.3 | async-start | bytes 7798784 | tf_op jit(solution)/shard_map/all_gather | solution.py:132
  7.9 432.1 %reduce-scatter.4.cloned.1.call-start = ((), (), s32[]{:S(2)}) async-start(), calls=%async_computation.4 | async-start | bytes 7798784 | tf_op jit(solution)/shard_map/reduce_scatter | solution.py:159
  8.0 11.8 %collective-permute-start = (bf16[64,3584]{1,0:T(8,128)(2,1)}, bf16[64,3584]{1,0:T(8,128)(2,1)S(1)}, u32[]{:S(2)}, u32[]{:S(2)}) collective-permute-start(bf16[64,3584]{1,0:T(8,128)(2,1)} %param.8), channel_id=1, source_target_pairs={{0,15},{1,0},{2,1},{3,2},{4,3},{5,4},{6,5},{7,6},{8,7},{9,8},{10,9... | collective-permute-start | bytes 1376264 | tf_op jit(solution)/shard_map/ppermute | solution.py:127
  19.8 110.6 %copy-start.2 = (bf16[64,3584]{1,0:T(8,128)(2,1)}, bf16[64,3584]{1,0:T(8,128)(2,1)S(1)}, u32[]{:S(2)}) copy-start(bf16[64,3584]{1,0:T(8,128)(2,1)S(1)} %collective-permute-done) | copy-start | bytes 1376260
  21.1 34.0 %collective-permute-start.1 = (bf16[128,3584]{1,0:T(8,128)(2,1)S(1)}, bf16[128,3584]{1,0:T(8,128)(2,1)S(1)}, u32[]{:S(2)}, u32[]{:S(2)}) collective-permute-start(bf16[128,3584]{1,0:T(8,128)(2,1)S(1)} %pad_maximum_fusion.3), channel_id=1, source_target_pairs={{0,14},{1,15},{2,0},{3,1},{4,2},{5,3},{6,4},{7,5},{8,6},{9,7},{10,... | collective-permute-start | bytes 2752520 | tf_op jit(solution)/shard_map/ppermute | solution.py:127
  56.3 74.2 %copy-start.6 = (bf16[64,8]{0,1:T(8,128)(2,1)S(1)}, bf16[64,8]{0,1:T(8,128)(2,1)}, u32[]{:S(2)}) copy-start(bf16[64,8]{0,1:T(8,128)(2,1)} %param.11) | copy-start | bytes 3076
  56.3 74.2 %copy-start.5 = (s32[64,8]{0,1:T(8,128)S(1)}, s32[64,8]{0,1:T(8,128)}, u32[]{:S(2)}) copy-start(s32[64,8]{0,1:T(8,128)} %param.10) | copy-start | bytes 6148
  56.3 72.1 %collective-permute-start.2 = (bf16[256,3584]{1,0:T(8,128)(2,1)S(1)}, bf16[256,3584]{1,0:T(8,128)(2,1)S(1)}, u32[]{:S(2)}, u32[]{:S(2)}) collective-permute-start(bf16[256,3584]{1,0:T(8,128)(2,1)S(1)} %pad_maximum_fusion.2), channel_id=1, source_target_pairs={{0,12},{1,13},{2,14},{3,15},{4,0},{5,1},{6,2},{7,3},{8,4},{9,5},{1... | collective-permute-start | bytes 5505032 | tf_op jit(solution)/shard_map/ppermute | solution.py:127
  130.4 161.3 %collective-permute-start.3 = (bf16[512,3584]{1,0:T(8,128)(2,1)}, bf16[512,3584]{1,0:T(8,128)(2,1)}, u32[]{:S(2)}, u32[]{:S(2)}) collective-permute-start(bf16[512,3584]{1,0:T(8,128)(2,1)} %pad_maximum_fusion), channel_id=1, source_target_pairs={{0,8},{1,9},{2,10},{3,11},{4,12},{5,13},{6,14},{7,15},{8,0},{9,1},... | collective-permute-start | bytes 11010056 | tf_op jit(solution)/shard_map/ppermute | solution.py:127
  229.3 64.8 %copy-start.3 = (bf16[64,3584]{1,0:T(8,128)(2,1)S(1)}, bf16[64,3584]{1,0:T(8,128)(2,1)}, u32[]{:S(2)}) copy-start(bf16[64,3584]{1,0:T(8,128)(2,1)} %copy-done.2) | copy-start | bytes 1376260
  294.3 3.1 copy-start.9
  297.5 6.8 %copy-start.4 = (bf16[2048,3584]{1,0:T(8,128)(2,1)}, bf16[2048,3584]{1,0:T(8,128)(2,1)S(1)}, u32[]{:S(2)}) copy-start(bf16[2048,3584]{1,0:T(8,128)(2,1)S(1)} %constant_dynamic-update-slice_fusion) | copy-start | bytes 44040196
  297.5 6.8 %copy-start.7 = (bf16[1,3584,512]{2,1,0:T(8,128)(2,1)S(1)}, bf16[1,3584,512]{2,1,0:T(8,128)(2,1)}, u32[]{:S(2)}) copy-start(bf16[1,3584,512]{2,1,0:T(8,128)(2,1)} %param.12) | copy-start | bytes 11010052
  309.5 10.2 %copy-start.8 = (bf16[1,3584,512]{2,1,0:T(8,128)(2,1)S(1)}, bf16[1,3584,512]{2,1,0:T(8,128)(2,1)}, u32[]{:S(2)}) copy-start(bf16[1,3584,512]{2,1,0:T(8,128)(2,1)} %param.12) | copy-start | bytes 11010052
  319.7 7.3 %copy-start.10 = (bf16[1,3584,512]{2,1,0:T(8,128)(2,1)S(1)}, bf16[1,3584,512]{2,1,0:T(8,128)(2,1)}, u32[]{:S(2)}) copy-start(bf16[1,3584,512]{2,1,0:T(8,128)(2,1)} %param.13) | copy-start | bytes 11010052
  336.2 145.6 %reduce-scatter.8.cloned.1.call-start = ((), (), s32[]{:S(2)}) async-start(), calls=%async_computation.6 | async-start | bytes 4128768 | tf_op jit(solution)/shard_map/reduce_scatter | solution.py:171
  350.6 147.8 %reduce-scatter.6.cloned.1.call-start = ((), (), s32[]{:S(2)}) async-start(), calls=%async_computation.5 | async-start | bytes 688128 | tf_op jit(solution)/shard_map/reduce_scatter | solution.py:160
Sparse Core Ops, SparseCore 0:
  10.3 111.9 all-gather.2
  336.3 103.6 reduce-scatter.3
  442.9 38.8 reduce-scatter.7
  484.5 13.8 reduce-scatter.5
